TPU v7x, 128 devices: a whole 4x4x4 slice. The times are simulated.
128 devices in a mesh: row: 8 (over z_hi, x), col: 16 (over y, z_lo, core).
Axes of the slice: x: 4, y: 4, z: 4 (z_hi: 2, z_lo: 2; z = z_hi * 2 + z_lo), core: 2. Of those that a mesh axis runs over, the one named last changes fastest.
Arguments:
- kernel_blocks: bfloat16 [64, 8, 256, 256], P('col', 'row'), may hold values from -6 to 6
- row_intersection: bfloat16 [512, 256, 256], P('col'), may hold values from -0.375 to 0.375
- col_intersection: bfloat16 [32, 256, 256], P('row'), may hold values from -0.375 to 0.375
- trial: bfloat16 [32, 64, 256], P('row', 'col'), may hold values from -0.0625 to 0.0625
- coarse_of_row: int32 [512], replicated, may hold values from 0 to 63, as said below
Outputs:
- fine_kernel: bfloat16 [512, 32, 256, 256], P('col', 'row')
- applied: bfloat16 [512, 64, 256], P(('col', 'row'))
Inputs may be any that keep to these rules, and one draw needn't show every extreme that they name: coarse_of_row never falls from one fine point to the next; coarse point 0 starts at fine point 0, and coarse point j >= 1 starts at fine point j * 8 - 512 // 128 + e_j with e_j between -3 and 3; every coarse point takes 1 to 15 consecutive fine points, and the last takes exactly 15.
All inputs are finite; a program needn't handle non-finite values.
Results may differ from a plain program's by a relative error of at most 0.0057.
Values may be sent and summed in bfloat16 or wider, within the bound.
A program may use at most 128 MiB of HBM per device.

v0:
```python
import jax
import jax.numpy as jnp
from jax import lax
from jax.sharding import PartitionSpec as P


def from_behind(shard, axis, by):
    size = lax.axis_size(axis)
    pairs = [(i, i + by) for i in range(size) if 0 <= i + by < size]
    return lax.ppermute(shard, axis, pairs)


def per_device(kernel_blocks, row_intersection, col_intersection, trial, coarse_of_row):
    myself = lax.axis_index("col")
    rows_dev = row_intersection.shape[0]
    nc_dev = kernel_blocks.shape[0]
    owned = lax.dynamic_slice_in_dim(coarse_of_row, myself * rows_dev, rows_dev)
    local_blocks = kernel_blocks[:, 0]
    following = from_behind(local_blocks[0:1], "col", -1)
    available = jnp.concatenate([local_blocks, following], axis=0)
    right_avail = jnp.einsum(
        "nab,jbc->njac", available, col_intersection, preferred_element_type=jnp.float32
    ).astype(jnp.bfloat16)
    position = jnp.clip(owned - myself * nc_dev, 0, nc_dev)
    right = right_avail[position]
    fine_kernel = jnp.einsum(
        "kba,kjbc->kjac", row_intersection, right, preferred_element_type=jnp.float32
    ).astype(jnp.bfloat16)
    full_trial = lax.all_gather(trial, "col", axis=1, tiled=True)
    share = rows_dev // lax.axis_size("row")
    whole_sum = lax.psum(
        jnp.einsum("kjab,jvb->kva", fine_kernel, full_trial, preferred_element_type=jnp.float32),
        "row",
    )
    summed = lax.dynamic_slice_in_dim(whole_sum, lax.axis_index("row") * share, share, 0)
    applied = summed.astype(jnp.bfloat16)
    return (fine_kernel, applied)


def solution(mesh):
    in_specs = (
        P("col", "row", None, None),
        P("col", None, None),
        P("row", None, None),
        P("row", "col", None),
        P(),
    )
    out_specs = (P("col", "row", None, None), P(("col", "row"), None, None))
    return jax.shard_map(
        per_device, mesh=mesh, in_specs=in_specs, out_specs=out_specs, check_vma=False
    )
```

profile of v0, /device:TPU:0, one launch (start us, length us, event | category | flops | bytes accessed | tf_op | source)
XLA Modules:
  0.0 167.4 jit_solution(6421750058855469775)
XLA Ops:
  0.6 0.0 copy-start
  0.6 1.0 slice_bitcast_fusion
  1.6 1.3 collective-permute-start
  2.9 0.7 copy.13
  3.6 0.8 compare_select_fusion
  4.4 21.4 %all_gather.3 = bf16[4,64,256]{2,0,1:T(4,128)(2,1)S(1)} all-gather(bf16[4,4,256]{2,0,1:T(4,128)(2,1)S(1)} %copy.13), channel_id=1, replica_groups=mesh['row'=8,'col'=16] {'col'}, dimensions={1}, use_global_device_ids=true | all-gather | bytes 139264 | tf_op jit(solution)/shard_map/all_gather | solution.py:29
  25.7 0.0 collective-permute-done
  25.8 0.0 copy-done
  25.8 1.9 %convert_bitcast_fusion.1 = bf16[5,4,256,256]{3,2,1,0:T(8,128)(2,1)S(1)} fusion(bf16[1,256,256]{2,1,0:T(8,128)(2,1)S(1)} %collective-permute-done, bf16[4,256,256]{2,1,0:T(8,128)(2,1)} %bitcast.30, bf16[4,256,256]{2,1,0:T(8,128)(2,1)S(1)} %copy-done), kind=kOutput, calls=%fused_computation.3 | convolution fusion | flops 673710080 | bytes 3801088 | tf_op jit(solution)/shard_map/nab,jbc->njac/dot_general | solution.py:21
  27.7 7.5 %gather_fusion = bf16[32,4,256,256]{3,2,1,0:T(8,128)(2,1)} fusion(bf16[5,4,256,256]{3,2,1,0:T(8,128)(2,1)S(1)} %convert_bitcast_fusion.1, s32[1024]{0:T(1024)S(1)} %pad_clamp_fusion), kind=kCustom, calls=%fused_computation | custom fusion | bytes 33554560 | tf_op jit(solution)/shard_map/gather | solution.py:25
  35.1 14.5 %convert_bitcast_fusion = bf16[32,4,256,256]{2,3,1,0:T(8,128)(2,1)} fusion(bf16[32,4,256,256]{3,2,1,0:T(8,128)(2,1)} %gather_fusion, bf16[32,256,256]{2,1,0:T(8,128)(2,1)} %param.6), kind=kOutput, calls=%fused_computation.1 | convolution fusion | flops 4303355904 | bytes 37748736 | tf_op jit(solution)/shard_map/kba,kjbc->kjac/dot_general | solution.py:26
  49.6 22.5 %copy.16 = bf16[32,4,256,256]{3,2,1,0:T(8,128)(2,1)} copy(bf16[32,4,256,256]{2,3,1,0:T(8,128)(2,1)} %convert_bitcast_fusion) | data formatting | bytes 33554432
  72.0 8.8 %convolution_bitcast_fusion = f32[32,64,256]{2,1,0:T(8,128)S(1)} fusion(bf16[32,4,256,256]{2,3,1,0:T(8,128)(2,1)} %convert_bitcast_fusion, bf16[4,64,256]{2,0,1:T(4,128)(2,1)S(1)} %all_gather.3), kind=kOutput, calls=%fused_computation.4 | convolution fusion | flops 1073741824 | bytes 19005440 | tf_op jit(solution)/shard_map/kjab,jvb->kva/dot_general | solution.py:32
  80.8 85.0 %all-reduce.1 = bf16[32,64,256]{2,1,0:T(8,128)(2,1)} all-reduce(f32[32,64,256]{2,1,0:T(8,128)S(1)} %convolution_bitcast_fusion), channel_id=1, replica_groups=mesh['row'=8,'col'=16] {'row'}, use_global_device_ids=true, to_apply=%region_0.1 | all-reduce | flops 524288 | bytes 3145728 | tf_op jit(solution)/shard_map/psum | solution.py:31
  165.8 1.6 dynamic-slice_convert_fusion
  (1 shorter events, 0.0 us)
Async XLA Ops:
  0.6 25.1 %copy-start = (bf16[4,256,256]{2,1,0:T(8,128)(2,1)S(1)}, bf16[4,256,256]{2,1,0:T(8,128)(2,1)}, u32[]{:S(2)}) copy-start(bf16[4,256,256]{2,1,0:T(8,128)(2,1)} %param.7) | copy-start | bytes 1572868
  1.6 24.1 %collective-permute-start = (bf16[1,256,256]{2,1,0:T(8,128)(2,1)S(1)}, bf16[1,256,256]{2,1,0:T(8,128)(2,1)S(1)}, u32[]{:S(2)}, u32[]{:S(2)}) collective-permute-start(bf16[1,256,256]{2,1,0:T(8,128)(2,1)S(1)} %slice_bitcast_fusion), channel_id=1, source_target_pairs={{1,0},{2,1},{3,2},{4,3},{5,4},{6,5},{7,6},{8,7},{9,8},{10,9},{11,1... | collective-permute-start | bytes 393224 | tf_op jit(solution)/shard_map/ppermute | solution.py:10
where the time goes:
time: 168 us; the launch traced here: 167 us
  blocking collectives  106 us (63%)
  local copies, waits for them, and re-layouts  33.2 us (20%)
  matrix products  25.1 us (15%)
    psum x1, blocking collectives, per_device(): lax.psum(jnp.einsum('kjab,jvb->kva', fine_kernel, full_trial, preferred_e...  85 us
    unnamed x4, local copies, waits for them, and re-layouts  23.2 us
    all_gather x1, blocking collectives, per_device(): full_trial = lax.all_gather(trial, 'col', axis=1, tiled=True)  21.4 us
    dot_general x1, matrix products, per_device(): jnp.einsum('kba,kjbc->kjac', row_intersection, right, preferred_element_t...  14.5 us
    dot_general x1, matrix products, per_device(): jnp.einsum('kjab,jvb->kva', fine_kernel, full_trial, preferred_element_ty...  8.78 us
    gather x1, local copies, waits for them, and re-layouts, per_device(): right = right_avail[position]  7.46 us
  transfers between devices with their start and end apart: 1, of which 0 were waited for; matrix products, arithmetic and copies ran while one was open for 1% of the time, Pallas kernels for 0%

commit v1 on v0

v1 whole, which is shorter than its diff:
```python
import jax
import jax.numpy as jnp
from jax import lax
from jax.experimental import pallas as pl
from jax.experimental.pallas import tpu as pltpu
from jax.sharding import PartitionSpec as P

MESH = pl.DeviceIdType.MESH
BF = jnp.bfloat16
F32 = jnp.float32
NROW, NCOL = 8, 16
S = 256
NV = 64
KD = 32
MD = 4
NB = 5


def split_halves(x):
    high = x.astype(BF)
    return high, (x - high.astype(F32)).astype(BF)


def dot_t(x, y):
    return lax.dot_general(x, y, (((1,), (1,)), ((), ())), preferred_element_type=F32)


def exchange(
    kb_ref, ci_ref, tr_ref, right_ref, w_ref,
    kbuf, cbuf, tbuf, ypart, ybuf, pbuf, wbuf,
    lsem, ksend, krecv, ysend, yrecv, wsend, wrecv,
):
    r = lax.axis_index("row")
    c = lax.axis_index("col")

    load_t = pltpu.make_async_copy(tr_ref, tbuf, lsem.at[0])
    load_c = pltpu.make_async_copy(ci_ref, cbuf, lsem.at[1])
    load_k = pltpu.make_async_copy(kb_ref.at[:, 0], kbuf.at[pl.ds(0, 4)], lsem.at[2])
    load_t.start()
    load_c.start()
    load_k.start()

    barrier = pltpu.get_barrier_semaphore()

    @pl.loop(1, NCOL)
    def _(off):
        pl.semaphore_signal(barrier, inc=1, device_id={"col": lax.rem(c + off, NCOL)}, device_id_type=MESH)

    @pl.loop(1, NROW)
    def _(off):
        pl.semaphore_signal(barrier, inc=1, device_id={"row": lax.rem(r + off, NROW)}, device_id_type=MESH)

    load_t.wait()
    load_c.wait()
    y = dot_t(tbuf[0], cbuf[0])
    for m in range(1, MD):
        y += dot_t(tbuf[m], cbuf[m])
    high, low = split_halves(y)
    both = jnp.concatenate([high.astype(F32), low.astype(F32)], axis=0).astype(BF)
    ypart[...] = both
    ybuf[c] = both
    load_k.wait()

    pl.semaphore_wait(barrier, NCOL + NROW - 2)

    def k_copy():
        return pltpu.make_async_remote_copy(
            src_ref=kbuf.at[0], dst_ref=kbuf.at[4], send_sem=ksend, recv_sem=krecv,
            device_id={"col": lax.rem(c + NCOL - 1, NCOL)}, device_id_type=MESH,
        )

    def y_copy(off):
        return pltpu.make_async_remote_copy(
            src_ref=ypart, dst_ref=ybuf.at[c], send_sem=ysend.at[off], recv_sem=yrecv.at[c],
            device_id={"col": lax.rem(c + off, NCOL)}, device_id_type=MESH,
        )

    def y_arrival(off):
        return pltpu.make_async_remote_copy(
            src_ref=ypart, dst_ref=ybuf.at[lax.rem(c + off, NCOL)], send_sem=ysend.at[off],
            recv_sem=yrecv.at[lax.rem(c + off, NCOL)],
            device_id={"col": lax.rem(c + off, NCOL)}, device_id_type=MESH,
        )

    @pl.loop(1, NCOL)
    def _(off):
        y_copy(off).start()

    k_copy().start()

    @pl.loop(0, 4)
    def _(p):
        for m in range(MD):
            right_ref[p, :, m * S:(m + 1) * S] = jnp.dot(
                kbuf[p], cbuf[m], preferred_element_type=F32
            ).astype(BF)

    @pl.loop(1, NCOL)
    def _(off):
        y_arrival(off).wait_recv()

    yall = ybuf[...].astype(F32).reshape(NCOL * 8, S).astype(BF)

    def partial(p):
        x = dot_t(yall, kbuf[p]).reshape(NCOL // 2, 2, 8, S)
        x = x + jnp.concatenate([x[:, :, 4:], x[:, :, :4]], axis=2)
        first = lax.broadcasted_iota(jnp.int32, (NCOL // 2, 8, S), 1) < 4
        return jnp.where(first, x[:, 0], x[:, 1]).reshape(NV, S)

    k_copy().wait_recv()

    @pl.loop(0, NB)
    def _(p):
        pbuf[p] = partial(p).astype(BF)

    def w_copy(off):
        d = lax.rem(r + off, NROW)
        return pltpu.make_async_remote_copy(
            src_ref=pbuf.at[pl.ds(d // 2, 2)], dst_ref=wbuf.at[r], send_sem=wsend.at[off], recv_sem=wrecv.at[r],
            device_id={"row": d}, device_id_type=MESH,
        )

    def w_arrival(off):
        d = lax.rem(r + off, NROW)
        return pltpu.make_async_remote_copy(
            src_ref=pbuf.at[pl.ds(d // 2, 2)], dst_ref=wbuf.at[d], send_sem=wsend.at[off], recv_sem=wrecv.at[d],
            device_id={"row": d}, device_id_type=MESH,
        )

    @pl.loop(1, NROW)
    def _(off):
        w_copy(off).start()

    for m in range(MD):
        right_ref[4, :, m * S:(m + 1) * S] = jnp.dot(kbuf[4], cbuf[m], preferred_element_type=F32).astype(BF)
    wbuf[r] = pbuf[pl.ds(r // 2, 2)]

    k_copy().wait_send()

    @pl.loop(1, NCOL)
    def _(off):
        y_copy(off).wait_send()

    @pl.loop(1, NROW)
    def _(off):
        w_arrival(off).wait_recv()

    total = wbuf[0].astype(F32)
    for i in range(1, NROW):
        total += wbuf[i].astype(F32)
    w_ref[...] = total

    @pl.loop(1, NROW)
    def _(off):
        w_copy(off).wait_send()


def expand(cor_ref, row_ref, right_ref, w_ref, fine_ref, app_ref, wsplit):
    step = pl.program_id(0)
    r = lax.axis_index("row")
    c = lax.axis_index("col")
    position = jnp.clip(cor_ref[c * KD + step] - c * 4, 0, NB - 1)
    rows = row_ref[0]
    out = lax.dot_general(
        rows, right_ref[position], (((0,), (0,)), ((), ())), preferred_element_type=F32
    ).astype(BF)
    for m in range(MD):
        fine_ref[0, m] = out[:, m * S:(m + 1) * S]

    @pl.when(step == 0)
    def _():
        for i in range(2):
            high, low = split_halves(w_ref[i])
            wsplit[i, :NV] = high
            wsplit[i, NV:] = low

    @pl.when(step // 4 == r)
    def _():
        which = jnp.clip(position - r // 2, 0, 1)
        x = jnp.dot(wsplit[which], rows, preferred_element_type=F32)
        app_ref[step % 4] = (x[:NV] + x[NV:]).astype(BF)


def per_device(kernel_blocks, row_intersection, col_intersection, trial, coarse_of_row):
    hbm_spec = pl.BlockSpec(memory_space=pltpu.HBM)
    vmem_spec = pl.BlockSpec(memory_space=pltpu.VMEM)
    right, w = pl.pallas_call(
        exchange,
        out_shape=(jax.ShapeDtypeStruct((NB, S, MD * S), BF), jax.ShapeDtypeStruct((2, NV, S), F32)),
        in_specs=[hbm_spec, hbm_spec, hbm_spec],
        out_specs=(vmem_spec, vmem_spec),
        scratch_shapes=[
            pltpu.VMEM((NB, S, S), BF),
            pltpu.VMEM((MD, S, S), BF),
            pltpu.VMEM((MD, 4, S), BF),
            pltpu.VMEM((8, S), BF),
            pltpu.VMEM((NCOL, 8, S), BF),
            pltpu.VMEM((NB, NV, S), BF),
            pltpu.VMEM((NROW, 2, NV, S), BF),
            pltpu.SemaphoreType.DMA((3,)),
            pltpu.SemaphoreType.DMA,
            pltpu.SemaphoreType.DMA,
            pltpu.SemaphoreType.DMA((NCOL,)),
            pltpu.SemaphoreType.DMA((NCOL,)),
            pltpu.SemaphoreType.DMA((NROW,)),
            pltpu.SemaphoreType.DMA((NROW,)),
        ],
        compiler_params=pltpu.CompilerParams(
            collective_id=0, has_side_effects=True, vmem_limit_bytes=16 << 20
        ),
        name="exchange",
    )(kernel_blocks, col_intersection, trial)

    return pl.pallas_call(
        expand,
        out_shape=(jax.ShapeDtypeStruct((KD, MD, S, S), BF), jax.ShapeDtypeStruct((4, NV, S), BF)),
        grid_spec=pltpu.PrefetchScalarGridSpec(
            num_scalar_prefetch=1,
            grid=(KD,),
            in_specs=[
                pl.BlockSpec((1, S, S), lambda k, cor: (k, 0, 0)),
                pl.BlockSpec((NB, S, MD * S), lambda k, cor: (0, 0, 0), pipeline_mode=pl.Buffered(1)),
                pl.BlockSpec((2, NV, S), lambda k, cor: (0, 0, 0), pipeline_mode=pl.Buffered(1)),
            ],
            out_specs=(
                pl.BlockSpec((1, MD, S, S), lambda k, cor: (k, 0, 0, 0)),
                pl.BlockSpec((4, NV, S), lambda k, cor: (0, 0, 0)),
            ),
            scratch_shapes=[pltpu.VMEM((2, 2 * NV, S), BF)],
        ),
        compiler_params=pltpu.CompilerParams(
            dimension_semantics=("arbitrary",), vmem_limit_bytes=16 << 20
        ),
        name="expand",
    )(coarse_of_row, row_intersection, right, w)


def solution(mesh):
    in_specs = (
        P("col", "row", None, None),
        P("col", None, None),
        P("row", None, None),
        P("row", "col", None),
        P(),
    )
    out_specs = (P("col", "row", None, None), P(("col", "row"), None, None))
    return jax.shard_map(
        per_device, mesh=mesh, in_specs=in_specs, out_specs=out_specs, check_vma=False
    )
```

time: 168 us -> 48 us (0.29)
  blocking collectives: 106 us -> 0 us
  Pallas kernels: 0 us -> 41 us
  local copies, waits for them, and re-layouts: 33.2 us -> 5.64 us
  matrix products: 25.1 us -> 0 us
    psum x1 -> x0, blocking collectives: 85 us -> none  [per_device(): lax.psum(jnp.einsum('kjab,jvb->kva', fine_kernel, full_trial, preferred_e...]
    pallas_call x0 -> x2, Pallas kernels: none -> 41 us  [the longest x1 21.7 us: per_device(): pl.pallas_call(exchange, out_shape=(jax.ShapeDtypeStruct((NB, S, MD * S),...]
    dot_general x3 -> x0, matrix products: 25.1 us -> none  [the longest x1 14.5 us: per_device(): jnp.einsum('kba,kjbc->kjac', row_intersection, right, preferred_element_t...]
    all_gather x1 -> x0, blocking collectives: 21.4 us -> none  [per_device(): full_trial = lax.all_gather(trial, 'col', axis=1, tiled=True)]
    unnamed x4 -> x10, local copies, waits for them, and re-layouts: 23.2 us -> 5.64 us
    gather x1 -> x0, local copies, waits for them, and re-layouts: 7.46 us -> none  [per_device(): right = right_avail[position]]
  transfers between devices with their start and end apart: 1 -> 0, of which waited for: 0 -> 0; matrix products, arithmetic and copies ran while one was open for 1% -> 0% of each run, Pallas kernels for 0% -> 0%
where the time goes in v1:
time: 48 us; the launch traced here: 47.3 us
  Pallas kernels  41 us (85%)
  local copies, waits for them, and re-layouts  5.64 us (12%)
  between operations  0.66 us (1%)
    pallas_call x1, Pallas kernels, per_device(): pl.pallas_call(exchange, out_shape=(jax.ShapeDtypeStruct((NB, S, MD * S),...  21.7 us
    pallas_call x1, Pallas kernels, per_device(): pl.pallas_call(expand, out_shape=(jax.ShapeDtypeStruct((KD, MD, S, S), BF...  19.4 us
    unnamed x10, local copies, waits for them, and re-layouts  5.64 us

profile of v1, /device:TPU:0, one launch (start us, length us, event | category | flops | bytes accessed | tf_op | source)
XLA Modules:
  0.0 47.3 jit_solution(15690694601804884422)
XLA Ops:
  0.6 0.0 copy-start.1
  0.6 1.0 %copy-done.1 = bf16[4,1,256,256]{3,2,1,0:T(8,128)(2,1)S(1)} copy-done((bf16[4,1,256,256]{3,2,1,0:T(8,128)(2,1)S(1)}, bf16[4,1,256,256]{3,2,1,0:T(8,128)(2,1)}, u32[]{:S(2)}) %copy-start.1) | copy-done | bytes 524312
  1.7 0.0 copy-start.2
  1.7 1.0 %copy-done.2 = bf16[4,256,256]{2,1,0:T(8,128)(2,1)S(1)} copy-done((bf16[4,256,256]{2,1,0:T(8,128)(2,1)S(1)}, bf16[4,256,256]{2,1,0:T(8,128)(2,1)}, u32[]{:S(2)}) %copy-start.2) | copy-done | bytes 524312
  2.7 0.0 copy-start.3
  2.7 0.7 %copy-done.3 = bf16[4,4,256]{2,1,0:T(4,128)(2,1)S(1)} copy-done((bf16[4,4,256]{2,1,0:T(4,128)(2,1)S(1)}, bf16[4,4,256]{2,1,0:T(4,128)(2,1)}, u32[]{:S(2)}) %copy-start.3) | copy-done | bytes 8216
  3.4 21.7 %exchange.1 = (bf16[5,256,1024]{2,1,0:T(8,128)(2,1)S(1)}, f32[2,64,256]{2,1,0:T(8,128)S(1)}) custom-call(bf16[4,1,256,256]{3,2,1,0:T(8,128)(2,1)S(1)} %copy-done.1, bf16[4,256,256]{2,1,0:T(8,128)(2,1)S(1)} %copy-done.2, bf16[4,4,256]{2,1,0:T(4,128)(2,1)S(1)} %copy-done.3), custom_call_target="tpu_custom_call" | custom-call | tf_op jit(solution)/shard_map/exchange/pallas_call | solution.py:187
  25.1 0.0 copy-start
  25.1 2.2 %copy-done = bf16[32,256,256]{2,1,0:T(8,128)(2,1)S(1)} copy-done((bf16[32,256,256]{2,1,0:T(8,128)(2,1)S(1)}, bf16[32,256,256]{2,1,0:T(8,128)(2,1)}, u32[]{:S(2)}) %copy-start) | copy-done | bytes 4194328
  27.3 0.0 copy-start.4
  27.3 0.7 %copy-done.4 = s32[512]{0:T(512)S(1)} copy-done((s32[512]{0:T(512)S(1)}, s32[512]{0:T(512)}, u32[]{:S(2)}) %copy-start.4) | copy-done | bytes 2072
  28.0 19.4 %expand.1 = (bf16[32,4,256,256]{3,2,1,0:T(8,128)(2,1)}, bf16[4,64,256]{2,1,0:T(8,128)(2,1)}) custom-call(s32[512]{0:T(512)S(1)} %copy-done.4, bf16[32,256,256]{2,1,0:T(8,128)(2,1)S(1)} %copy-done, bf16[5,256,1024]{2,1,0:T(8,128)(2,1)S(1)} %get-tuple-element.4.right_ref, f32[2,64,256]{2,1,0:T(8,128)S(1)} %get-tuple-element.5.w_ref), custom_call_target="tpu_custom_call" | custom-call | tf_op jit(solution)/shard_map/expand/pallas_call | solution.py:214
Async XLA Ops:
  0.6 1.0 %copy-start.1 = (bf16[4,1,256,256]{3,2,1,0:T(8,128)(2,1)S(1)}, bf16[4,1,256,256]{3,2,1,0:T(8,128)(2,1)}, u32[]{:S(2)}) copy-start(bf16[4,1,256,256]{3,2,1,0:T(8,128)(2,1)} %kb_ref.1) | copy-start | bytes 1572868
  1.7 1.0 %copy-start.2 = (bf16[4,256,256]{2,1,0:T(8,128)(2,1)S(1)}, bf16[4,256,256]{2,1,0:T(8,128)(2,1)}, u32[]{:S(2)}) copy-start(bf16[4,256,256]{2,1,0:T(8,128)(2,1)} %ci_ref.1) | copy-start | bytes 1572868
  2.7 0.7 %copy-start.3 = (bf16[4,4,256]{2,1,0:T(4,128)(2,1)S(1)}, bf16[4,4,256]{2,1,0:T(4,128)(2,1)}, u32[]{:S(2)}) copy-start(bf16[4,4,256]{2,1,0:T(4,128)(2,1)} %tr_ref.1) | copy-start | bytes 24580
  25.1 2.2 %copy-start = (bf16[32,256,256]{2,1,0:T(8,128)(2,1)S(1)}, bf16[32,256,256]{2,1,0:T(8,128)(2,1)}, u32[]{:S(2)}) copy-start(bf16[32,256,256]{2,1,0:T(8,128)(2,1)} %row_ref.1) | copy-start | bytes 12582916
  27.3 0.7 %copy-start.4 = (s32[512]{0:T(512)S(1)}, s32[512]{0:T(512)}, u32[]{:S(2)}) copy-start(s32[512]{0:T(512)} %cor_ref.1) | copy-start | bytes 6148

commit v2 on v0

v2 whole, which is shorter than its diff:
```python
import jax
import jax.numpy as jnp
from jax import lax
from jax.experimental import pallas as pl
from jax.experimental.pallas import tpu as pltpu
from jax.sharding import PartitionSpec as P

MESH = pl.DeviceIdType.MESH
BF = jnp.bfloat16
F32 = jnp.float32
NROW, NCOL = 8, 16
S = 256
NV = 64
KD = 32
MD = 4
NB = 5
CUTS = (0, 8, 10, 20)
EARLY = CUTS[-1]
NEAR = 48
COL_ORDER = [(dy, dj) for dy in (2, 1, 3, 0) for dj in range(4) if dy or dj]
ROW_ORDER = [(1, 2), (1, 1), (1, 3), (1, 0), (0, 2), (0, 1), (0, 3)]


def split_halves(x):
    high = x.astype(BF)
    return high, (x - high.astype(F32)).astype(BF)


def fine_block(rows, right):
    return lax.dot_general(rows, right, (((0,), (0,)), ((), ())), preferred_element_type=F32).astype(BF)


def remote(src, dst, send_sem, recv_sem, **device):
    return pltpu.make_async_remote_copy(
        src_ref=src, dst_ref=dst, send_sem=send_sem, recv_sem=recv_sem, device_id=device, device_id_type=MESH
    )


def exchange(
    cor_ref, kb_ref, ci_ref, tr_ref, row_ref, fine_ref, right_ref, rows_ref, w_ref,
    cor, kbuf, kt, cbuf, tbuf, ypart, ybuf, pbuf, wbuf,
    lsem, ksend, krecv, ysend, yrecv, wsend, wrecv,
):
    r = lax.axis_index("row")
    c = lax.axis_index("col")
    y, j = c // 4, lax.rem(c, 4)

    load_t = pltpu.make_async_copy(tr_ref, tbuf, lsem.at[0])
    load_c = pltpu.make_async_copy(ci_ref, cbuf, lsem.at[1])
    load_k = pltpu.make_async_copy(kb_ref.at[:, 0], kbuf.at[pl.ds(0, 4)], lsem.at[2])
    load_p = pltpu.make_async_copy(cor_ref, cor, lsem.at[3])
    load_r = pltpu.make_async_copy(row_ref, rows_ref, lsem.at[4])
    load_t.start()
    load_c.start()
    load_k.start()

    col_peers = [lax.rem(y + dy, 4) * 4 + lax.rem(j + dj, 4) for dy, dj in COL_ORDER]
    row_peers = [lax.rem(r // 4 + dz, 2) * 4 + lax.rem(lax.rem(r, 4) + dx, 4) for dz, dx in ROW_ORDER]
    barrier = pltpu.get_barrier_semaphore()
    for peer in row_peers:
        pl.semaphore_signal(barrier, inc=1, device_id={"row": peer}, device_id_type=MESH)
    for peer in col_peers:
        pl.semaphore_signal(barrier, inc=1, device_id={"col": peer}, device_id_type=MESH)
    load_p.start()
    load_r.start()

    load_t.wait()
    load_c.wait()
    part = None
    for m in range(MD):
        x = lax.dot_general(tbuf[m], cbuf[m], (((1,), (1,)), ((), ())), preferred_element_type=F32)
        part = x if part is None else part + x
    high, low = split_halves(part)
    both = jnp.concatenate([high.astype(F32), low.astype(F32)], axis=0).astype(BF)
    ypart[...] = both
    ybuf[1, j] = both
    load_k.wait()

    def right_block(p):
        for m in range(MD):
            right_ref[p, :, m * S:(m + 1) * S] = jnp.dot(kbuf[p], cbuf[m], preferred_element_type=F32).astype(BF)

    @pl.loop(0, 4)
    def _(p):
        kt[p] = kbuf[p].T
        right_block(p)

    pl.semaphore_wait(barrier, NCOL + NROW - 2)

    k_copy = remote(kbuf.at[0], kbuf.at[4], ksend, krecv, col=lax.rem(c + NCOL - 1, NCOL))
    y_copies = []
    for i, ((dy, dj), peer) in enumerate(zip(COL_ORDER, col_peers)):
        slot = (1 - dy) % 4
        y_copies.append(remote(ypart, ybuf.at[slot, j], ysend.at[i], yrecv.at[slot, j], col=peer))
    for copy in y_copies:
        copy.start()
    k_copy.start()

    def wait_y(slots):
        for slot in slots:
            for dj in range(4):
                if slot != 1 or dj:
                    other = lax.rem(j + dj, 4)
                    remote(ypart, ybuf.at[slot, other], ysend.at[0], yrecv.at[slot, other], col=c).wait_recv()

    def fine_range(start, stop):
        @pl.loop(start, stop, step=2)
        def _(k):
            for i in range(2):
                position = jnp.clip(cor[c * KD + k + i] - c * 4, 0, NB - 1)
                out = fine_block(rows_ref[k + i], right_ref[position])
                for m in range(MD):
                    fine_ref[k + i, m] = out[:, m * S:(m + 1) * S]

    def partial(left, p):
        n = left.shape[0] // 16
        x = jnp.dot(left, kt[p], preferred_element_type=F32).reshape(n, 2, 8, S)
        x = x + jnp.concatenate([x[:, :, 4:], x[:, :, :4]], axis=2)
        first = lax.broadcasted_iota(jnp.int32, (n, 8, S), 1) < 4
        return jnp.where(first, x[:, 0], x[:, 1]).reshape(n * 8, S).astype(BF)

    load_p.wait()
    load_r.wait()
    fine_range(CUTS[0], CUTS[1])

    wait_y((1, 0, 2))
    left_near = ybuf[0:3].astype(F32).reshape(96, S).astype(BF)
    for p in range(4):
        pbuf[p, 0:NEAR] = partial(left_near, p)

    for i, d in enumerate(row_peers):
        q = d // 2

        @pl.when(q < 3)
        def _():
            remote(
                pbuf.at[pl.ds(q, 2), pl.ds(0, NEAR)], wbuf.at[r, :, pl.ds(0, NEAR)], wsend.at[i], wrecv.at[r], row=d
            ).start()

        @pl.when(q == 3)
        def _():
            remote(
                pbuf.at[3, pl.ds(0, NEAR)], wbuf.at[r, 0, pl.ds(0, NEAR)], wsend.at[i], wrecv.at[r], row=d
            ).start()

    fine_range(CUTS[1], CUTS[2])
    k_copy.wait_recv()
    kt[4] = kbuf[4].T
    pbuf[4, 0:NEAR] = partial(left_near, 4)

    wait_y((3,))
    left_far = ybuf[3].astype(F32).reshape(32, S).astype(BF)
    for p in range(NB):
        pbuf[p, NEAR:] = partial(left_far, p)

    for i, d in enumerate(row_peers):
        q = d // 2

        @pl.when(q < 3)
        def _():
            remote(
                pbuf.at[pl.ds(q, 2), pl.ds(NEAR, NV - NEAR)], wbuf.at[r, :, pl.ds(NEAR, NV - NEAR)],
                wsend.at[i], wrecv.at[r], row=d,
            ).start()

        @pl.when(q == 3)
        def _():
            remote(pbuf.at[4], wbuf.at[r, 1], wsend.at[i], wrecv.at[r], row=d).start()
            remote(
                pbuf.at[3, pl.ds(NEAR, NV - NEAR)], wbuf.at[r, 0, pl.ds(NEAR, NV - NEAR)],
                wsend.at[i], wrecv.at[r], row=d,
            ).start()

    right_block(4)
    fine_range(CUTS[2], CUTS[3])

    k_copy.wait_send()
    for copy in y_copies:
        copy.wait_send()
    total = pbuf[pl.ds(r // 2, 2)].astype(F32)
    for d in reversed(row_peers):
        remote(wbuf.at[d], wbuf.at[d], wsend.at[0], wrecv.at[d], row=d).wait_recv()
        total += wbuf[d].astype(F32)
    for slot in range(4):
        w_ref[:, lax.rem(y + 3 + slot, 4)] = total[:, slot * 16:(slot + 1) * 16]
    for i, d in enumerate(row_peers):
        remote(pbuf.at[pl.ds(d // 2, 2)], wbuf.at[d], wsend.at[i], wrecv.at[d], row=d).wait_send()


def finish(
    cor_ref, early_ref, right_ref, rows_ref, w_ref, fine_ref, app_ref, cor, late, app, wsplit, sem, esem, lsem, asem
):
    r = lax.axis_index("row")
    c = lax.axis_index("col")
    load_p = pltpu.make_async_copy(cor_ref, cor, sem)
    load_p.start()
    early = [
        pltpu.make_async_copy(early_ref.at[pl.ds(i * 4, 4)], fine_ref.at[pl.ds(i * 4, 4)], esem.at[i])
        for i in range(EARLY // 4)
    ]
    for copy in early:
        copy.start()
    for i in range(2):
        high, low = split_halves(w_ref[i].reshape(NV, S))
        wsplit[i, :NV] = high
        wsplit[i, NV:] = low
    load_p.wait()

    def position_of(k):
        return jnp.clip(cor[c * KD + k] - c * 4, 0, NB - 1)

    def late_copy(k):
        return pltpu.make_async_copy(late.at[pl.ds(k, 2)], fine_ref.at[pl.ds(EARLY + k, 2)], lsem.at[k // 2])

    @pl.loop(0, KD - EARLY, step=2)
    def _(k):
        for i in range(2):
            out = fine_block(rows_ref[EARLY + k + i], right_ref[position_of(EARLY + k + i)])
            for m in range(MD):
                late[k + i, m] = out[:, m * S:(m + 1) * S]
        late_copy(k).start()

    for i in range(4):
        k = r * 4 + i
        which = jnp.clip(position_of(k) - r // 2, 0, 1)
        x = jnp.dot(wsplit[which], rows_ref[k], preferred_element_type=F32)
        app[i] = (x[:NV] + x[NV:]).astype(BF)
    app_copy = pltpu.make_async_copy(app, app_ref, asem)
    app_copy.start()

    for copy in early:
        copy.wait()

    @pl.loop(0, KD - EARLY, step=2)
    def _(k):
        late_copy(k).wait()

    app_copy.wait()


def per_device(kernel_blocks, row_intersection, col_intersection, trial, coarse_of_row):
    hbm_spec = pl.BlockSpec(memory_space=pltpu.HBM)
    vmem_spec = pl.BlockSpec(memory_space=pltpu.VMEM)
    arrays = (coarse_of_row, kernel_blocks, col_intersection, trial, row_intersection)
    arrays = [pltpu.with_memory_space_constraint(x, pltpu.HBM) for x in arrays]
    early, right, rows, w = pl.pallas_call(
        exchange,
        out_shape=(
            jax.ShapeDtypeStruct((EARLY, MD, S, S), BF),
            jax.ShapeDtypeStruct((NB, S, MD * S), BF),
            jax.ShapeDtypeStruct((KD, S, S), BF),
            jax.ShapeDtypeStruct((2, 4, 16, S), F32),
        ),
        in_specs=[hbm_spec] * 5,
        out_specs=(vmem_spec,) * 4,
        scratch_shapes=[
            pltpu.SMEM((NCOL * KD,), jnp.int32),
            pltpu.VMEM((NB, S, S), BF),
            pltpu.VMEM((NB, S, S), BF),
            pltpu.VMEM((MD, S, S), BF),
            pltpu.VMEM((MD, 4, S), BF),
            pltpu.VMEM((8, S), BF),
            pltpu.VMEM((4, 4, 8, S), BF),
            pltpu.VMEM((NB, NV, S), BF),
            pltpu.VMEM((NROW, 2, NV, S), BF),
            pltpu.SemaphoreType.DMA((5,)),
            pltpu.SemaphoreType.DMA,
            pltpu.SemaphoreType.DMA,
            pltpu.SemaphoreType.DMA((NCOL,)),
            pltpu.SemaphoreType.DMA((4, 4)),
            pltpu.SemaphoreType.DMA((NROW,)),
            pltpu.SemaphoreType.DMA((NROW,)),
        ],
        compiler_params=pltpu.CompilerParams(
            collective_id=0, has_side_effects=True, vmem_limit_bytes=28 << 20
        ),
        name="exchange",
    )(*arrays)

    return pl.pallas_call(
        finish,
        out_shape=(jax.ShapeDtypeStruct((KD, MD, S, S), BF), jax.ShapeDtypeStruct((4, NV, S), BF)),
        in_specs=[hbm_spec] + [vmem_spec] * 4,
        out_specs=(hbm_spec, hbm_spec),
        scratch_shapes=[
            pltpu.SMEM((NCOL * KD,), jnp.int32),
            pltpu.VMEM((KD - EARLY, MD, S, S), BF),
            pltpu.VMEM((4, NV, S), BF),
            pltpu.VMEM((2, 2 * NV, S), BF),
            pltpu.SemaphoreType.DMA,
            pltpu.SemaphoreType.DMA((EARLY // 4,)),
            pltpu.SemaphoreType.DMA(((KD - EARLY) // 2,)),
            pltpu.SemaphoreType.DMA,
        ],
        compiler_params=pltpu.CompilerParams(vmem_limit_bytes=28 << 20),
        name="finish",
    )(arrays[0], early, right, rows, w)


def solution(mesh):
    in_specs = (
        P("col", "row", None, None),
        P("col", None, None),
        P("row", None, None),
        P("row", "col", None),
        P(),
    )
    out_specs = (P("col", "row", None, None), P(("col", "row"), None, None))
    return jax.shard_map(
        per_device, mesh=mesh, in_specs=in_specs, out_specs=out_specs, check_vma=False
    )
```

time: 168 us -> 28.9 us (0.17)
  blocking collectives: 106 us -> 0 us
  local copies, waits for them, and re-layouts: 33.2 us -> 0 us
  Pallas kernels: 0 us -> 27.9 us
  matrix products: 25.1 us -> 0 us
    psum x1 -> x0, blocking collectives: 85 us -> none  [per_device(): lax.psum(jnp.einsum('kjab,jvb->kva', fine_kernel, full_trial, preferred_e...]
    pallas_call x0 -> x2, Pallas kernels: none -> 27.9 us  [the longest x1 21.9 us: per_device(): pl.pallas_call(exchange, out_shape=(jax.ShapeDtypeStruct((EARLY, MD, S, S...]
    dot_general x3 -> x0, matrix products: 25.1 us -> none  [the longest x1 14.5 us: per_device(): jnp.einsum('kba,kjbc->kjac', row_intersection, right, preferred_element_t...]
    unnamed x4 -> x0, local copies, waits for them, and re-layouts: 23.2 us -> none
    all_gather x1 -> x0, blocking collectives: 21.4 us -> none  [per_device(): full_trial = lax.all_gather(trial, 'col', axis=1, tiled=True)]
    gather x1 -> x0, local copies, waits for them, and re-layouts: 7.46 us -> none  [per_device(): right = right_avail[position]]
  transfers between devices with their start and end apart: 1 -> 0, of which waited for: 0 -> 0; matrix products, arithmetic and copies ran while one was open for 1% -> 0% of each run, Pallas kernels for 0% -> 0%
where the time goes in v2:
time: 28.9 us; the launch traced here: 28.5 us
  Pallas kernels  27.9 us (97%)
  between operations  0.64 us (2%)
    pallas_call x1, Pallas kernels, per_device(): pl.pallas_call(exchange, out_shape=(jax.ShapeDtypeStruct((EARLY, MD, S, S...  21.9 us
    pallas_call x1, Pallas kernels, per_device(): pl.pallas_call(finish, out_shape=(jax.ShapeDtypeStruct((KD, MD, S, S), BF...  5.94 us

profile of v2, /device:TPU:0, one launch (start us, length us, event | category | flops | bytes accessed | tf_op | source)
XLA Modules:
  0.0 28.5 jit_solution(13308124511713165800)
XLA Ops:
  0.6 21.9 %exchange.1 = (bf16[20,4,256,256]{3,2,1,0:T(8,128)(2,1)S(1)}, bf16[5,256,1024]{2,1,0:T(8,128)(2,1)S(1)}, bf16[32,256,256]{2,1,0:T(8,128)(2,1)S(1)}, f32[2,4,16,256]{3,2,1,0:T(8,128)S(1)}) custom-call(s32[512]{0:T(512)} %cor_ref.3, bf16[4,1,256,256]{3,2,1,0:T(8,128)(2,1)} %kb_ref.1, bf16[4,256,256]{2,1,0:T(8,128)(2,1)} %ci_ref.1, bf16[4,4,256]{2,1,0:T(4,128)(2,1)} %tr_ref.1, ...), custom_call_target="tpu_custom_call" | custom-call | tf_op jit(solution)/shard_map/exchange/pallas_call | solution.py:246
  22.6 5.9 %finish.1 = (bf16[32,4,256,256]{3,2,1,0:T(8,128)(2,1)}, bf16[4,64,256]{2,1,0:T(8,128)(2,1)}) custom-call(s32[512]{0:T(512)} %cor_ref.3, bf16[20,4,256,256]{3,2,1,0:T(8,128)(2,1)S(1)} %get-tuple-element.6.early_ref, bf16[5,256,1024]{2,1,0:T(8,128)(2,1)S(1)} %get-tuple-element.7.right_ref, bf16[32,256,256]{2,1,0:T(8,128)(2,1)S(1)} %get-tuple-element.8.rows_ref, ...), custom_call_target="tpu_custom_call" | custom-call | tf_op jit(solution)/shard_map/finish/pallas_call | solution.py:280

commit v3 on v2

--- a/solution.py
+++ b/solution.py
@@ -14,11 +14,18 @@
 KD = 32
 MD = 4
 NB = 5
-CUTS = (0, 8, 10, 20)
+CUTS = (0, 4, 8, 16)
 EARLY = CUTS[-1]
-NEAR = 48
-COL_ORDER = [(dy, dj) for dy in (2, 1, 3, 0) for dj in range(4) if dy or dj]
-ROW_ORDER = [(1, 2), (1, 1), (1, 3), (1, 0), (0, 2), (0, 1), (0, 3)]
+NEAR = 56
+UNITS = ((0, 0), (3, 0), (1, 0), (0, 1), (2, 0), (3, 1), (1, 1), (2, 1))
+COL_ORDER = [
+    (dy, flip, dc)
+    for dy, flip in ((2, 1), (1, 1), (3, 1), (2, 0), (0, 1), (1, 0), (3, 0), (0, 0))
+    for dc in range(2)
+    if dy or flip or dc
+]
+X_ORDER = (2, 1, 3)
+ROW_ORDER = ((1, 2), (1, 1), (1, 3), (1, 0), (0, 2), (0, 1), (0, 3))
 
 
 def split_halves(x):
@@ -38,12 +45,12 @@
 
 def exchange(
     cor_ref, kb_ref, ci_ref, tr_ref, row_ref, fine_ref, right_ref, rows_ref, w_ref,
-    cor, kbuf, kt, cbuf, tbuf, ypart, ybuf, pbuf, wbuf,
-    lsem, ksend, krecv, ysend, yrecv, wsend, wrecv,
+    cor, kbuf, kt, cbuf, tbuf, ypart, ybuf, pwide, pbuf, zbuf, sbuf, xbuf, fbuf,
+    lsem, ksend, krecv, ysend, yrecv, zsend, zrecv, xsend, xrecv, fsend, frecv,
 ):
     r = lax.axis_index("row")
     c = lax.axis_index("col")
-    y, j = c // 4, lax.rem(c, 4)
+    y, zlo, core = c // 4, lax.rem(c // 2, 2), lax.rem(c, 2)
 
     load_t = pltpu.make_async_copy(tr_ref, tbuf, lsem.at[0])
     load_c = pltpu.make_async_copy(ci_ref, cbuf, lsem.at[1])
@@ -54,9 +61,14 @@
     load_c.start()
     load_k.start()
 
-    col_peers = [lax.rem(y + dy, 4) * 4 + lax.rem(j + dj, 4) for dy, dj in COL_ORDER]
-    row_peers = [lax.rem(r // 4 + dz, 2) * 4 + lax.rem(lax.rem(r, 4) + dx, 4) for dz, dx in ROW_ORDER]
+    col_peers = [
+        lax.rem(y + dy, 4) * 4 + lax.rem(zlo + flip, 2) * 2 + lax.rem(core + dc, 2) for dy, flip, dc in COL_ORDER
+    ]
+    half, x = r // 4, lax.rem(r, 4)
+    z_peer = (1 - half) * 4 + x
+    x_peers = [lax.rem(x + dx, 4) for dx in X_ORDER]
     barrier = pltpu.get_barrier_semaphore()
+    row_peers = [lax.rem(half + dz, 2) * 4 + lax.rem(x + dx, 4) for dz, dx in ROW_ORDER]
     for peer in row_peers:
         pl.semaphore_signal(barrier, inc=1, device_id={"row": peer}, device_id_type=MESH)
     for peer in col_peers:
@@ -68,40 +80,40 @@
     load_c.wait()
     part = None
     for m in range(MD):
-        x = lax.dot_general(tbuf[m], cbuf[m], (((1,), (1,)), ((), ())), preferred_element_type=F32)
-        part = x if part is None else part + x
+        term = lax.dot_general(tbuf[m], cbuf[m], (((1,), (1,)), ((), ())), preferred_element_type=F32)
+        part = term if part is None else part + term
     high, low = split_halves(part)
     both = jnp.concatenate([high.astype(F32), low.astype(F32)], axis=0).astype(BF)
     ypart[...] = both
-    ybuf[1, j] = both
+    ybuf[0, core] = both
     load_k.wait()
 
     def right_block(p):
         for m in range(MD):
             right_ref[p, :, m * S:(m + 1) * S] = jnp.dot(kbuf[p], cbuf[m], preferred_element_type=F32).astype(BF)
+
+    pl.semaphore_wait(barrier, NCOL + NROW - 2)
+
+    k_copy = remote(kbuf.at[0], kbuf.at[4], ksend, krecv, col=lax.rem(c + NCOL - 1, NCOL))
+    y_copies = []
+    for i, ((dy, flip, _), peer) in enumerate(zip(COL_ORDER, col_peers)):
+        unit = UNITS.index((-dy % 4, flip))
+        y_copies.append(remote(ypart, ybuf.at[unit, core], ysend.at[i], yrecv.at[unit, core], col=peer))
+    for copy in y_copies:
+        copy.start()
+    k_copy.start()
 
     @pl.loop(0, 4)
     def _(p):
         kt[p] = kbuf[p].T
         right_block(p)
 
-    pl.semaphore_wait(barrier, NCOL + NROW - 2)
-
-    k_copy = remote(kbuf.at[0], kbuf.at[4], ksend, krecv, col=lax.rem(c + NCOL - 1, NCOL))
-    y_copies = []
-    for i, ((dy, dj), peer) in enumerate(zip(COL_ORDER, col_peers)):
-        slot = (1 - dy) % 4
-        y_copies.append(remote(ypart, ybuf.at[slot, j], ysend.at[i], yrecv.at[slot, j], col=peer))
-    for copy in y_copies:
-        copy.start()
-    k_copy.start()
-
-    def wait_y(slots):
-        for slot in slots:
-            for dj in range(4):
-                if slot != 1 or dj:
-                    other = lax.rem(j + dj, 4)
-                    remote(ypart, ybuf.at[slot, other], ysend.at[0], yrecv.at[slot, other], col=c).wait_recv()
+    def wait_y(start, stop):
+        for unit in range(start, stop):
+            for dc in range(2):
+                if unit or dc:
+                    other = lax.rem(core + dc, 2)
+                    remote(ypart, ybuf.at[unit, other], ysend.at[0], yrecv.at[unit, other], col=c).wait_recv()
 
     def fine_range(start, stop):
         @pl.loop(start, stop, step=2)
@@ -112,64 +124,69 @@
                 for m in range(MD):
                     fine_ref[k + i, m] = out[:, m * S:(m + 1) * S]
 
-    def partial(left, p):
-        n = left.shape[0] // 16
-        x = jnp.dot(left, kt[p], preferred_element_type=F32).reshape(n, 2, 8, S)
-        x = x + jnp.concatenate([x[:, :, 4:], x[:, :, :4]], axis=2)
+    def partial(start, stop, blocks):
+        left = ybuf[start:stop].astype(F32).reshape((stop - start) * 16, S).astype(BF)
+        n = stop - start
         first = lax.broadcasted_iota(jnp.int32, (n, 8, S), 1) < 4
-        return jnp.where(first, x[:, 0], x[:, 1]).reshape(n * 8, S).astype(BF)
+        for p in blocks:
+            both = jnp.dot(left, kt[p], preferred_element_type=F32).reshape(n, 2, 8, S)
+            both = both + jnp.concatenate([both[:, :, 4:], both[:, :, :4]], axis=2)
+            wide = jnp.where(first, both[:, 0], both[:, 1]).reshape(n * 8, S)
+            pwide[p, start * 8:stop * 8] = wide
+            pbuf[p, start * 8:stop * 8] = wide.astype(BF)
+
+    near, far = pl.ds(0, NEAR), pl.ds(NEAR, NV - NEAR)
+    sent = 2 - 2 * half
+
+    def z_copy(i, src, dst):
+        return remote(src, dst, zsend.at[i], zrecv.at[i], row=z_peer)
+
+    z_copies = [
+        z_copy(0, pbuf.at[pl.ds(sent, 2), near], zbuf.at[pl.ds(0, 2)]),
+        z_copy(1, pbuf.at[sent + 2, near], zbuf.at[2]),
+    ]
+    far_copies = [
+        remote(pbuf.at[pl.ds(peer // 2, 2), far], fbuf.at[r], fsend.at[i], frecv.at[r], row=peer)
+        for i, peer in enumerate(row_peers)
+    ]
+
+    def add_halves(i):
+        sbuf[i] = (pwide[2 * half + i, :NEAR] + zbuf[i].astype(F32)).astype(BF)
+
+    def send_x(place, blocks, dst):
+        for i, other in enumerate(x_peers):
+
+            @pl.when(other // 2 == place)
+            def _():
+                remote(blocks, dst, xsend.at[i], xrecv.at[x], row=half * 4 + other).start()
 
     load_p.wait()
     load_r.wait()
+
+    wait_y(0, 7)
+    partial(0, 7, range(4))
+    z_copies[0].start()
     fine_range(CUTS[0], CUTS[1])
 
-    wait_y((1, 0, 2))
-    left_near = ybuf[0:3].astype(F32).reshape(96, S).astype(BF)
-    for p in range(4):
-        pbuf[p, 0:NEAR] = partial(left_near, p)
-
-    for i, d in enumerate(row_peers):
-        q = d // 2
-
-        @pl.when(q < 3)
-        def _():
-            remote(
-                pbuf.at[pl.ds(q, 2), pl.ds(0, NEAR)], wbuf.at[r, :, pl.ds(0, NEAR)], wsend.at[i], wrecv.at[r], row=d
-            ).start()
-
-        @pl.when(q == 3)
-        def _():
-            remote(
-                pbuf.at[3, pl.ds(0, NEAR)], wbuf.at[r, 0, pl.ds(0, NEAR)], wsend.at[i], wrecv.at[r], row=d
-            ).start()
-
-    fine_range(CUTS[1], CUTS[2])
     k_copy.wait_recv()
     kt[4] = kbuf[4].T
-    pbuf[4, 0:NEAR] = partial(left_near, 4)
-
-    wait_y((3,))
-    left_far = ybuf[3].astype(F32).reshape(32, S).astype(BF)
-    for p in range(NB):
-        pbuf[p, NEAR:] = partial(left_far, p)
-
-    for i, d in enumerate(row_peers):
-        q = d // 2
-
-        @pl.when(q < 3)
-        def _():
-            remote(
-                pbuf.at[pl.ds(q, 2), pl.ds(NEAR, NV - NEAR)], wbuf.at[r, :, pl.ds(NEAR, NV - NEAR)],
-                wsend.at[i], wrecv.at[r], row=d,
-            ).start()
-
-        @pl.when(q == 3)
-        def _():
-            remote(pbuf.at[4], wbuf.at[r, 1], wsend.at[i], wrecv.at[r], row=d).start()
-            remote(
-                pbuf.at[3, pl.ds(NEAR, NV - NEAR)], wbuf.at[r, 0, pl.ds(NEAR, NV - NEAR)],
-                wsend.at[i], wrecv.at[r], row=d,
-            ).start()
+    partial(0, 7, (4,))
+    z_copies[1].start()
+
+    wait_y(7, 8)
+    partial(7, 8, range(NB))
+    for copy in far_copies:
+        copy.start()
+    fine_range(CUTS[1], CUTS[2])
+
+    z_copies[0].wait_recv()
+    add_halves(0)
+    add_halves(1)
+    send_x(0, sbuf.at[pl.ds(0, 2)], xbuf.at[x])
+    send_x(1, sbuf.at[1], xbuf.at[x, 0])
+    z_copies[1].wait_recv()
+    add_halves(2)
+    send_x(1, sbuf.at[2], xbuf.at[x, 1])
 
     right_block(4)
     fine_range(CUTS[2], CUTS[3])
@@ -177,14 +194,28 @@
     k_copy.wait_send()
     for copy in y_copies:
         copy.wait_send()
-    total = pbuf[pl.ds(r // 2, 2)].astype(F32)
-    for d in reversed(row_peers):
-        remote(wbuf.at[d], wbuf.at[d], wsend.at[0], wrecv.at[d], row=d).wait_recv()
-        total += wbuf[d].astype(F32)
-    for slot in range(4):
-        w_ref[:, lax.rem(y + 3 + slot, 4)] = total[:, slot * 16:(slot + 1) * 16]
-    for i, d in enumerate(row_peers):
-        remote(pbuf.at[pl.ds(d // 2, 2)], wbuf.at[d], wsend.at[i], wrecv.at[d], row=d).wait_send()
+    for copy in z_copies:
+        copy.wait_send()
+    total = sbuf[pl.ds(x // 2, 2)].astype(F32)
+    for other in reversed(x_peers):
+        remote(xbuf.at[other], xbuf.at[other], xsend.at[0], xrecv.at[other], row=r).wait_recv()
+        total += xbuf[other].astype(F32)
+
+    def place(i):
+        dy, flip = UNITS[i]
+        return lax.rem(y + dy, 4) * 2 + lax.rem(zlo + flip, 2)
+
+    for i in range(7):
+        w_ref[:, place(i)] = total[:, i * 8:(i + 1) * 8]
+    last = pwide[pl.ds(r // 2, 2), NEAR:]
+    for peer in reversed(row_peers):
+        remote(fbuf.at[peer], fbuf.at[peer], fsend.at[0], frecv.at[peer], row=r).wait_recv()
+        last += fbuf[peer].astype(F32)
+    w_ref[:, place(7)] = last
+    for i, other in enumerate(x_peers):
+        remote(xbuf.at[other], xbuf.at[other], xsend.at[i], xrecv.at[other], row=r).wait_send()
+    for copy in far_copies:
+        copy.wait_send()
 
 
 def finish(
@@ -249,7 +280,7 @@
             jax.ShapeDtypeStruct((EARLY, MD, S, S), BF),
             jax.ShapeDtypeStruct((NB, S, MD * S), BF),
             jax.ShapeDtypeStruct((KD, S, S), BF),
-            jax.ShapeDtypeStruct((2, 4, 16, S), F32),
+            jax.ShapeDtypeStruct((2, 8, 8, S), F32),
         ),
         in_specs=[hbm_spec] * 5,
         out_specs=(vmem_spec,) * 4,
@@ -260,14 +291,22 @@
             pltpu.VMEM((MD, S, S), BF),
             pltpu.VMEM((MD, 4, S), BF),
             pltpu.VMEM((8, S), BF),
-            pltpu.VMEM((4, 4, 8, S), BF),
+            pltpu.VMEM((8, 2, 8, S), BF),
+            pltpu.VMEM((NB, NV, S), F32),
             pltpu.VMEM((NB, NV, S), BF),
-            pltpu.VMEM((NROW, 2, NV, S), BF),
+            pltpu.VMEM((3, NEAR, S), BF),
+            pltpu.VMEM((3, NEAR, S), BF),
+            pltpu.VMEM((4, 2, NEAR, S), BF),
+            pltpu.VMEM((NROW, 2, NV - NEAR, S), BF),
             pltpu.SemaphoreType.DMA((5,)),
             pltpu.SemaphoreType.DMA,
             pltpu.SemaphoreType.DMA,
             pltpu.SemaphoreType.DMA((NCOL,)),
-            pltpu.SemaphoreType.DMA((4, 4)),
+            pltpu.SemaphoreType.DMA((8, 2)),
+            pltpu.SemaphoreType.DMA((2,)),
+            pltpu.SemaphoreType.DMA((2,)),
+            pltpu.SemaphoreType.DMA((3,)),
+            pltpu.SemaphoreType.DMA((4,)),
             pltpu.SemaphoreType.DMA((NROW,)),
             pltpu.SemaphoreType.DMA((NROW,)),
         ],

time: 28.9 us -> 27 us (0.934)
  Pallas kernels: 27.9 us -> 26.2 us
    pallas_call x1, Pallas kernels: 21.9 us -> 20.2 us  [per_device(): pl.pallas_call(exchange, out_shape=(jax.ShapeDtypeStruct((EARLY, MD, S, S...]
where the time goes in v3:
time: 27 us; the launch traced here: 26.8 us
  Pallas kernels  26.2 us (97%)
  between operations  0.64 us (2%)
    pallas_call x1, Pallas kernels, per_device(): pl.pallas_call(exchange, out_shape=(jax.ShapeDtypeStruct((EARLY, MD, S, S...  20.2 us
    pallas_call x1, Pallas kernels, per_device(): pl.pallas_call(finish, out_shape=(jax.ShapeDtypeStruct((KD, MD, S, S), BF...  5.95 us

profile of v3, /device:TPU:0, one launch (start us, length us, event | category | flops | bytes accessed | tf_op | source)
XLA Modules:
  0.0 26.8 jit_solution(1555376777579562806)
XLA Ops:
  0.6 20.2 %exchange.1 = (bf16[16,4,256,256]{3,2,1,0:T(8,128)(2,1)S(1)}, bf16[5,256,1024]{2,1,0:T(8,128)(2,1)S(1)}, bf16[32,256,256]{2,1,0:T(8,128)(2,1)S(1)}, f32[2,8,8,256]{3,2,1,0:T(8,128)S(1)}) custom-call(s32[512]{0:T(512)} %cor_ref.3, bf16[4,1,256,256]{3,2,1,0:T(8,128)(2,1)} %kb_ref.1, bf16[4,256,256]{2,1,0:T(8,128)(2,1)} %ci_ref.1, bf16[4,4,256]{2,1,0:T(4,128)(2,1)} %tr_ref.1, ...), custom_call_target="tpu_custom_call" | custom-call | tf_op jit(solution)/shard_map/exchange/pallas_call | solution.py:277
  20.9 5.9 %finish.1 = (bf16[32,4,256,256]{3,2,1,0:T(8,128)(2,1)}, bf16[4,64,256]{2,1,0:T(8,128)(2,1)}) custom-call(s32[512]{0:T(512)} %cor_ref.3, bf16[16,4,256,256]{3,2,1,0:T(8,128)(2,1)S(1)} %get-tuple-element.6.early_ref, bf16[5,256,1024]{2,1,0:T(8,128)(2,1)S(1)} %get-tuple-element.7.right_ref, bf16[32,256,256]{2,1,0:T(8,128)(2,1)S(1)} %get-tuple-element.8.rows_ref, ...), custom_call_target="tpu_custom_call" | custom-call | tf_op jit(solution)/shard_map/finish/pallas_call | solution.py:319

commit v4 on v3

--- a/solution.py
+++ b/solution.py
@@ -14,9 +14,12 @@
 KD = 32
 MD = 4
 NB = 5
-CUTS = (0, 4, 8, 16)
+CUTS = (0, 2, 4, 6, 16)
 EARLY = CUTS[-1]
+FIRST = 12
+BEGUN = 4
 NEAR = 56
+PARTS = ((0, 3), (3, 5), (5, 7))
 UNITS = ((0, 0), (3, 0), (1, 0), (0, 1), (2, 0), (3, 1), (1, 1), (2, 1))
 COL_ORDER = [
     (dy, flip, dc)
@@ -43,8 +46,57 @@
     )
 
 
+def first_count(r, c):
+    return jnp.where((r == 0) & (c < 2), BEGUN, 0)
+
+
+def store_block(ref, k, rows, right):
+    out = fine_block(rows, right)
+    for m in range(MD):
+        ref[k, m] = out[:, m * S:(m + 1) * S]
+
+
+def begin(cor_ref, kb_ref, ci_ref, row_ref, fine_ref, token_ref, cor, kbuf, cbuf, rows, right, blocks, lsem, wsem):
+    c = lax.axis_index("col")
+    count = first_count(lax.axis_index("row"), c)
+    token_ref[...] = jnp.zeros_like(token_ref)
+
+    @pl.when(count > 0)
+    def _():
+        load_k = pltpu.make_async_copy(kb_ref.at[pl.ds(0, 2), 0], kbuf, lsem.at[0])
+        load_c = pltpu.make_async_copy(ci_ref, cbuf, lsem.at[1])
+        load_p = pltpu.make_async_copy(cor_ref, cor, lsem.at[2])
+        load_r = pltpu.make_async_copy(row_ref.at[pl.ds(0, BEGUN)], rows, lsem.at[3])
+        for copy in (load_k, load_c, load_p, load_r):
+            copy.start()
+        load_k.wait()
+        load_c.wait()
+
+        @pl.loop(0, 2)
+        def _(p):
+            for m in range(MD):
+                right[p, :, m * S:(m + 1) * S] = jnp.dot(kbuf[p], cbuf[m], preferred_element_type=F32).astype(BF)
+
+        load_p.wait()
+        load_r.wait()
+
+        def block_copy(k):
+            return pltpu.make_async_copy(blocks.at[pl.ds(k, 2)], fine_ref.at[pl.ds(k, 2)], wsem.at[k // 2])
+
+        @pl.loop(0, BEGUN, step=2)
+        def _(k):
+            for i in range(2):
+                position = jnp.clip(cor[c * KD + k + i] - c * 4, 0, 1)
+                store_block(blocks, k + i, rows[k + i], right[position])
+            block_copy(k).start()
+
+        @pl.loop(0, BEGUN, step=2)
+        def _(k):
+            block_copy(k).wait()
+
+
 def exchange(
-    cor_ref, kb_ref, ci_ref, tr_ref, row_ref, fine_ref, right_ref, rows_ref, w_ref,
+    token_ref, cor_ref, kb_ref, ci_ref, tr_ref, row_ref, fine_ref, right_ref, rows_ref, w_ref,
     cor, kbuf, kt, cbuf, tbuf, ypart, ybuf, pwide, pbuf, zbuf, sbuf, xbuf, fbuf,
     lsem, ksend, krecv, ysend, yrecv, zsend, zrecv, xsend, xrecv, fsend, frecv,
 ):
@@ -119,10 +171,8 @@
         @pl.loop(start, stop, step=2)
         def _(k):
             for i in range(2):
-                position = jnp.clip(cor[c * KD + k + i] - c * 4, 0, NB - 1)
-                out = fine_block(rows_ref[k + i], right_ref[position])
-                for m in range(MD):
-                    fine_ref[k + i, m] = out[:, m * S:(m + 1) * S]
+                position = jnp.clip(cor[c * KD + FIRST + k + i] - c * 4, 0, NB - 1)
+                store_block(fine_ref, k + i, rows_ref[FIRST + k + i], right_ref[position])
 
     def partial(start, stop, blocks):
         left = ybuf[start:stop].astype(F32).reshape((stop - start) * 16, S).astype(BF)
@@ -142,16 +192,17 @@
         return remote(src, dst, zsend.at[i], zrecv.at[i], row=z_peer)
 
     z_copies = [
-        z_copy(0, pbuf.at[pl.ds(sent, 2), near], zbuf.at[pl.ds(0, 2)]),
-        z_copy(1, pbuf.at[sent + 2, near], zbuf.at[2]),
+        z_copy(i, pbuf.at[pl.ds(sent, 2), rows], zbuf.at[pl.ds(0, 2), rows])
+        for i, rows in enumerate(pl.ds(a * 8, (b - a) * 8) for a, b in PARTS)
     ]
+    z_copies.append(z_copy(len(PARTS), pbuf.at[sent + 2, near], zbuf.at[2]))
     far_copies = [
         remote(pbuf.at[pl.ds(peer // 2, 2), far], fbuf.at[r], fsend.at[i], frecv.at[r], row=peer)
         for i, peer in enumerate(row_peers)
     ]
 
-    def add_halves(i):
-        sbuf[i] = (pwide[2 * half + i, :NEAR] + zbuf[i].astype(F32)).astype(BF)
+    def add_halves(i, start, stop):
+        sbuf[i, start:stop] = (pwide[2 * half + i, start:stop] + zbuf[i, start:stop].astype(F32)).astype(BF)
 
     def send_x(place, blocks, dst):
         for i, other in enumerate(x_peers):
@@ -163,15 +214,16 @@
     load_p.wait()
     load_r.wait()
 
-    wait_y(0, 7)
-    partial(0, 7, range(4))
-    z_copies[0].start()
+    for i, (a, b) in enumerate(PARTS):
+        wait_y(a, b)
+        partial(a, b, range(4))
+        z_copies[i].start()
     fine_range(CUTS[0], CUTS[1])
 
     k_copy.wait_recv()
     kt[4] = kbuf[4].T
     partial(0, 7, (4,))
-    z_copies[1].start()
+    z_copies[-1].start()
 
     wait_y(7, 8)
     partial(7, 8, range(NB))
@@ -179,17 +231,21 @@
         copy.start()
     fine_range(CUTS[1], CUTS[2])
 
-    z_copies[0].wait_recv()
-    add_halves(0)
-    add_halves(1)
-    send_x(0, sbuf.at[pl.ds(0, 2)], xbuf.at[x])
-    send_x(1, sbuf.at[1], xbuf.at[x, 0])
-    z_copies[1].wait_recv()
-    add_halves(2)
+    for i, (a, b) in enumerate(PARTS):
+        z_copies[i].wait_recv()
+        add_halves(0, a * 8, b * 8)
+        add_halves(1, a * 8, b * 8)
+        rows = pl.ds(a * 8, (b - a) * 8)
+        send_x(0, sbuf.at[pl.ds(0, 2), rows], xbuf.at[x, :, rows])
+        send_x(1, sbuf.at[1, rows], xbuf.at[x, 0, rows])
+        if i == 0:
+            fine_range(CUTS[2], CUTS[3])
+    z_copies[-1].wait_recv()
+    add_halves(2, 0, NEAR)
     send_x(1, sbuf.at[2], xbuf.at[x, 1])
 
     right_block(4)
-    fine_range(CUTS[2], CUTS[3])
+    fine_range(CUTS[3], CUTS[4])
 
     k_copy.wait_send()
     for copy in y_copies:
@@ -219,14 +275,15 @@
 
 
 def finish(
-    cor_ref, early_ref, right_ref, rows_ref, w_ref, fine_ref, app_ref, cor, late, app, wsplit, sem, esem, lsem, asem
+    cor_ref, early_ref, right_ref, rows_ref, w_ref, begun_ref, fine_ref, app_ref,
+    cor, late, app, wsplit, sem, esem, lsem, asem,
 ):
     r = lax.axis_index("row")
     c = lax.axis_index("col")
     load_p = pltpu.make_async_copy(cor_ref, cor, sem)
     load_p.start()
     early = [
-        pltpu.make_async_copy(early_ref.at[pl.ds(i * 4, 4)], fine_ref.at[pl.ds(i * 4, 4)], esem.at[i])
+        pltpu.make_async_copy(early_ref.at[pl.ds(i * 4, 4)], fine_ref.at[pl.ds(FIRST + i * 4, 4)], esem.at[i])
         for i in range(EARLY // 4)
     ]
     for copy in early:
@@ -236,20 +293,21 @@
         wsplit[i, :NV] = high
         wsplit[i, NV:] = low
     load_p.wait()
+    count = first_count(r, c)
 
     def position_of(k):
         return jnp.clip(cor[c * KD + k] - c * 4, 0, NB - 1)
 
-    def late_copy(k):
-        return pltpu.make_async_copy(late.at[pl.ds(k, 2)], fine_ref.at[pl.ds(EARLY + k, 2)], lsem.at[k // 2])
-
-    @pl.loop(0, KD - EARLY, step=2)
-    def _(k):
+    def late_copy(slot):
+        k = slot + jnp.where(slot < FIRST, 0, EARLY)
+        return pltpu.make_async_copy(late.at[pl.ds(slot, 2)], fine_ref.at[pl.ds(k, 2)], lsem.at[slot // 2])
+
+    @pl.loop(count, KD - EARLY, step=2)
+    def _(slot):
         for i in range(2):
-            out = fine_block(rows_ref[EARLY + k + i], right_ref[position_of(EARLY + k + i)])
-            for m in range(MD):
-                late[k + i, m] = out[:, m * S:(m + 1) * S]
-        late_copy(k).start()
+            k = slot + i + jnp.where(slot < FIRST, 0, EARLY)
+            store_block(late, slot + i, rows_ref[k], right_ref[position_of(k)])
+        late_copy(slot).start()
 
     for i in range(4):
         k = r * 4 + i
@@ -262,9 +320,9 @@
     for copy in early:
         copy.wait()
 
-    @pl.loop(0, KD - EARLY, step=2)
-    def _(k):
-        late_copy(k).wait()
+    @pl.loop(count, KD - EARLY, step=2)
+    def _(slot):
+        late_copy(slot).wait()
 
     app_copy.wait()
 
@@ -274,6 +332,24 @@
     vmem_spec = pl.BlockSpec(memory_space=pltpu.VMEM)
     arrays = (coarse_of_row, kernel_blocks, col_intersection, trial, row_intersection)
     arrays = [pltpu.with_memory_space_constraint(x, pltpu.HBM) for x in arrays]
+    begun, token = pl.pallas_call(
+        begin,
+        out_shape=(jax.ShapeDtypeStruct((KD, MD, S, S), BF), jax.ShapeDtypeStruct((8, 128), F32)),
+        in_specs=[hbm_spec] * 4,
+        out_specs=(hbm_spec, vmem_spec),
+        scratch_shapes=[
+            pltpu.SMEM((NCOL * KD,), jnp.int32),
+            pltpu.VMEM((2, S, S), BF),
+            pltpu.VMEM((MD, S, S), BF),
+            pltpu.VMEM((BEGUN, S, S), BF),
+            pltpu.VMEM((2, S, MD * S), BF),
+            pltpu.VMEM((BEGUN, MD, S, S), BF),
+            pltpu.SemaphoreType.DMA((4,)),
+            pltpu.SemaphoreType.DMA((BEGUN // 2,)),
+        ],
+        compiler_params=pltpu.CompilerParams(vmem_limit_bytes=28 << 20),
+        name="begin",
+    )(arrays[0], arrays[1], arrays[2], arrays[4])
     early, right, rows, w = pl.pallas_call(
         exchange,
         out_shape=(
@@ -282,7 +358,7 @@
             jax.ShapeDtypeStruct((KD, S, S), BF),
             jax.ShapeDtypeStruct((2, 8, 8, S), F32),
         ),
-        in_specs=[hbm_spec] * 5,
+        in_specs=[pl.BlockSpec(memory_space=pl.ANY)] + [hbm_spec] * 5,
         out_specs=(vmem_spec,) * 4,
         scratch_shapes=[
             pltpu.SMEM((NCOL * KD,), jnp.int32),
@@ -303,8 +379,8 @@
             pltpu.SemaphoreType.DMA,
             pltpu.SemaphoreType.DMA((NCOL,)),
             pltpu.SemaphoreType.DMA((8, 2)),
-            pltpu.SemaphoreType.DMA((2,)),
-            pltpu.SemaphoreType.DMA((2,)),
+            pltpu.SemaphoreType.DMA((len(PARTS) + 1,)),
+            pltpu.SemaphoreType.DMA((len(PARTS) + 1,)),
             pltpu.SemaphoreType.DMA((3,)),
             pltpu.SemaphoreType.DMA((4,)),
             pltpu.SemaphoreType.DMA((NROW,)),
@@ -314,12 +390,12 @@
             collective_id=0, has_side_effects=True, vmem_limit_bytes=28 << 20
         ),
         name="exchange",
-    )(*arrays)
+    )(token, *arrays)
 
     return pl.pallas_call(
         finish,
         out_shape=(jax.ShapeDtypeStruct((KD, MD, S, S), BF), jax.ShapeDtypeStruct((4, NV, S), BF)),
-        in_specs=[hbm_spec] + [vmem_spec] * 4,
+        in_specs=[hbm_spec] + [vmem_spec] * 4 + [hbm_spec],
         out_specs=(hbm_spec, hbm_spec),
         scratch_shapes=[
             pltpu.SMEM((NCOL * KD,), jnp.int32),
@@ -332,8 +408,9 @@
             pltpu.SemaphoreType.DMA,
         ],
         compiler_params=pltpu.CompilerParams(vmem_limit_bytes=28 << 20),
+        input_output_aliases={5: 0},
         name="finish",
-    )(arrays[0], early, right, rows, w)
+    )(arrays[0], early, right, rows, w, begun)
 
 
 def solution(mesh):

time: 27 us -> 25.9 us (0.959)
  Pallas kernels: 26.2 us -> 25.1 us
    pallas_call x1, Pallas kernels: 20.2 us -> 16 us  [per_device(): pl.pallas_call(exchange, out_shape=(jax.ShapeDtypeStruct((EARLY, MD, S, S...]
    pallas_call x0 -> x1, Pallas kernels: none -> 3.7 us  [per_device(): pl.pallas_call(begin, out_shape=(jax.ShapeDtypeStruct((KD, MD, S, S), BF)...]
    pallas_call x1, Pallas kernels: 5.95 us -> 5.32 us  [per_device(): pl.pallas_call(finish, out_shape=(jax.ShapeDtypeStruct((KD, MD, S, S), BF...]
where the time goes in v4:
time: 25.9 us; the launch traced here: 25.7 us
  Pallas kernels  25.1 us (97%)
  between operations  0.64 us (2%)
    pallas_call x1, Pallas kernels, per_device(): pl.pallas_call(exchange, out_shape=(jax.ShapeDtypeStruct((EARLY, MD, S, S...  16 us
    pallas_call x1, Pallas kernels, per_device(): pl.pallas_call(finish, out_shape=(jax.ShapeDtypeStruct((KD, MD, S, S), BF...  5.32 us
    pallas_call x1, Pallas kernels, per_device(): pl.pallas_call(begin, out_shape=(jax.ShapeDtypeStruct((KD, MD, S, S), BF)...  3.7 us

profile of v4, /device:TPU:0, one launch (start us, length us, event | category | flops | bytes accessed | tf_op | source)
XLA Modules:
  0.0 25.7 jit_solution(15287869038470286321)
XLA Ops:
  0.6 3.7 %begin.1 = (bf16[32,4,256,256]{3,2,1,0:T(8,128)(2,1)}, f32[8,128]{1,0:T(8,128)S(1)}) custom-call(s32[512]{0:T(512)} %cor_ref.5, bf16[4,1,256,256]{3,2,1,0:T(8,128)(2,1)} %kb_ref.3, bf16[4,256,256]{2,1,0:T(8,128)(2,1)} %ci_ref.3, bf16[32,256,256]{2,1,0:T(8,128)(2,1)} %row_ref.3), custom_call_target="tpu_custom_call" | custom-call | tf_op jit(solution)/shard_map/begin/pallas_call | solution.py:335
  4.3 16.0 %exchange.1 = (bf16[16,4,256,256]{3,2,1,0:T(8,128)(2,1)S(1)}, bf16[5,256,1024]{2,1,0:T(8,128)(2,1)S(1)}, bf16[32,256,256]{2,1,0:T(8,128)(2,1)S(1)}, f32[2,8,8,256]{3,2,1,0:T(8,128)S(1)}) custom-call(f32[8,128]{1,0:T(8,128)S(1)} %get-tuple-element.8.token_ref, s32[512]{0:T(512)} %cor_ref.5, bf16[4,1,256,256]{3,2,1,0:T(8,128)(2,1)} %kb_ref.3, ...), custom_call_target="tpu_custom_call" | custom-call | tf_op jit(solution)/shard_map/exchange/pallas_call | solution.py:353
  20.4 5.3 %finish.1 = (bf16[32,4,256,256]{3,2,1,0:T(8,128)(2,1)}, bf16[4,64,256]{2,1,0:T(8,128)(2,1)}) custom-call(s32[512]{0:T(512)} %cor_ref.5, bf16[16,4,256,256]{3,2,1,0:T(8,128)(2,1)S(1)} %get-tuple-element.9.early_ref, bf16[5,256,1024]{2,1,0:T(8,128)(2,1)S(1)} %get-tuple-element.10.right_ref, ...), custom_call_target="tpu_custom_call", output_to_operand_aliasing={{0}: (5, {})} | custom-call | tf_op jit(solution)/shard_map/finish/pallas_call | solution.py:395

commit v5 on v4

--- a/solution.py
+++ b/solution.py
@@ -14,7 +14,7 @@
 KD = 32
 MD = 4
 NB = 5
-CUTS = (0, 2, 4, 6, 16)
+CUTS = (0, 2, 6, 6, 14)
 EARLY = CUTS[-1]
 FIRST = 12
 BEGUN = 4
@@ -283,8 +283,8 @@
     load_p = pltpu.make_async_copy(cor_ref, cor, sem)
     load_p.start()
     early = [
-        pltpu.make_async_copy(early_ref.at[pl.ds(i * 4, 4)], fine_ref.at[pl.ds(FIRST + i * 4, 4)], esem.at[i])
-        for i in range(EARLY // 4)
+        pltpu.make_async_copy(early_ref.at[pl.ds(i * 2, 2)], fine_ref.at[pl.ds(FIRST + i * 2, 2)], esem.at[i])
+        for i in range(EARLY // 2)
     ]
     for copy in early:
         copy.start()
@@ -403,7 +403,7 @@
             pltpu.VMEM((4, NV, S), BF),
             pltpu.VMEM((2, 2 * NV, S), BF),
             pltpu.SemaphoreType.DMA,
-            pltpu.SemaphoreType.DMA((EARLY // 4,)),
+            pltpu.SemaphoreType.DMA((EARLY // 2,)),
             pltpu.SemaphoreType.DMA(((KD - EARLY) // 2,)),
             pltpu.SemaphoreType.DMA,
         ],

time: 25.9 us -> 25.9 us (level)
  no operation moved by 1% of the time
where the time goes in v5:
time: 25.9 us; the launch traced here: 25.7 us
  Pallas kernels  25 us (97%)
  between operations  0.64 us (2%)
    pallas_call x1, Pallas kernels, per_device(): pl.pallas_call(exchange, out_shape=(jax.ShapeDtypeStruct((EARLY, MD, S, S...  16 us
    pallas_call x1, Pallas kernels, per_device(): pl.pallas_call(finish, out_shape=(jax.ShapeDtypeStruct((KD, MD, S, S), BF...  5.35 us
    pallas_call x1, Pallas kernels, per_device(): pl.pallas_call(begin, out_shape=(jax.ShapeDtypeStruct((KD, MD, S, S), BF)...  3.7 us

profile of v5, /device:TPU:0, one launch (start us, length us, event | category | flops | bytes accessed | tf_op | source)
XLA Modules:
  0.0 25.7 jit_solution(14112328761619394146)
XLA Ops:
  0.6 3.7 %begin.1 = (bf16[32,4,256,256]{3,2,1,0:T(8,128)(2,1)}, f32[8,128]{1,0:T(8,128)S(1)}) custom-call(s32[512]{0:T(512)} %cor_ref.5, bf16[4,1,256,256]{3,2,1,0:T(8,128)(2,1)} %kb_ref.3, bf16[4,256,256]{2,1,0:T(8,128)(2,1)} %ci_ref.3, bf16[32,256,256]{2,1,0:T(8,128)(2,1)} %row_ref.3), custom_call_target="tpu_custom_call" | custom-call | tf_op jit(solution)/shard_map/begin/pallas_call | solution.py:335
  4.3 16.0 %exchange.1 = (bf16[14,4,256,256]{3,2,1,0:T(8,128)(2,1)S(1)}, bf16[5,256,1024]{2,1,0:T(8,128)(2,1)S(1)}, bf16[32,256,256]{2,1,0:T(8,128)(2,1)S(1)}, f32[2,8,8,256]{3,2,1,0:T(8,128)S(1)}) custom-call(f32[8,128]{1,0:T(8,128)S(1)} %get-tuple-element.8.token_ref, s32[512]{0:T(512)} %cor_ref.5, bf16[4,1,256,256]{3,2,1,0:T(8,128)(2,1)} %kb_ref.3, ...), custom_call_target="tpu_custom_call" | custom-call | tf_op jit(solution)/shard_map/exchange/pallas_call | solution.py:353
  20.3 5.4 %finish.1 = (bf16[32,4,256,256]{3,2,1,0:T(8,128)(2,1)}, bf16[4,64,256]{2,1,0:T(8,128)(2,1)}) custom-call(s32[512]{0:T(512)} %cor_ref.5, bf16[14,4,256,256]{3,2,1,0:T(8,128)(2,1)S(1)} %get-tuple-element.9.early_ref, bf16[5,256,1024]{2,1,0:T(8,128)(2,1)S(1)} %get-tuple-element.10.right_ref, ...), custom_call_target="tpu_custom_call", output_to_operand_aliasing={{0}: (5, {})} | custom-call | tf_op jit(solution)/shard_map/finish/pallas_call | solution.py:395
